TPU v7x, 256 devices: a whole 4x4x8 slice. The times are simulated.
256 devices in a mesh: seq: 32 (over y, x, core), tp: 8 (over z).
Axes of the slice: x: 4, y: 4, z: 8, core: 2. Of those that a mesh axis runs over, the one named last changes fastest.
Arguments:
- tokens: bfloat16 [8192, 4096], P('seq', 'tp'), may hold values from -11 to 11
- grad_out: bfloat16 [8192, 4096], P('seq', 'tp'), may hold values from -1.5 to 1.5
- in_weight: bfloat16 [4096, 4096], P('seq', 'tp'), may hold values from -0.09880682 to 0.09880682
- in_scale: float32 [4096], P('tp'), may hold values from 0.0008238636 to 0.010511364
- out_weight: bfloat16 [4096, 4096], P('seq', 'tp'), may hold values from -0.053943182 to 0.053943182
- out_scale: float32 [4096], replicated, may hold values from 0.00139204545 to 0.0057386364
- state_in: bfloat16 [8192, 128], P('seq'), may hold values from -0.0625 to 0.0625
- state_out: bfloat16 [8192, 128], P('seq'), may hold values from -6 to 6
- log_decay: float32 [8192, 64], P('seq', 'tp'), may hold values from -1.6 to 0
Outputs:
- grad_tokens: bfloat16 [8192, 4096], P('seq', 'tp')
- grad_in_weight: float32 [4096, 4096], P('seq', 'tp')
- grad_in_scale: float32 [4096], P('tp')
- grad_out_weight: float32 [4096, 4096], P('seq', 'tp')
- grad_out_scale: float32 [4096], P('seq')
All inputs are finite; a program needn't handle non-finite values.
Results may differ from a plain program's by a relative error of at most 0.027.
Values may be sent and summed in bfloat16 or wider, within the bound.
No kernel may reach another device: no remote copies, remote signals or barrier semaphores. Data moves between devices by JAX's collectives and lax.ppermute only.
A program may use at most 128 MiB of HBM per device.

v0:
```python
import jax
import jax.numpy as jnp
from jax import lax
from jax.sharding import PartitionSpec as P

D = 4096
HEADS = 64
HEAD_DIM = 64
STRETCH = 256
QMAX = 7
precise = lax.Precision.HIGHEST


def prefix(array, axis, join, neutral, backward):
    count = lax.axis_size(axis)
    place = lax.axis_index(axis)
    ahead = count - 1 - place if backward else place
    gathered = jax.tree.map(
        lambda a, kind: lax.all_gather(a.astype(kind), axis), array, (jnp.bfloat16, jnp.bfloat16)
    )
    state = jax.tree.map(lambda a, e: jnp.zeros_like(a) + jnp.asarray(e, a.dtype), array, neutral)

    def one(turn, state):
        source = count - 1 - turn if backward else turn
        return join(
            state,
            jax.tree.map(
                lambda a, own: lax.dynamic_index_in_dim(a, source, 0, False).astype(own.dtype),
                gathered,
                array,
            ),
        )

    return lax.fori_loop(0, ahead, one, state)


def quantize(weight, channel_scale):
    ratios = weight.astype(jnp.float32) / channel_scale
    clipped = jnp.clip(ratios, -QMAX, QMAX)
    levels = jnp.floor(clipped + 0.5)
    inside = jnp.abs(ratios) <= QMAX
    slopes = jnp.where(inside, levels - ratios, levels)
    return (levels, slopes, inside.astype(jnp.float32))


def stretch_terms(decay_logs, inputs_f, outputs_f):
    cumul = jnp.cumsum(decay_logs, axis=0)
    ending = cumul[-1]
    spread = cumul[:, None, :] - cumul[None, :, :]
    length = decay_logs.shape[0]
    causal = jnp.arange(length)[:, None] >= jnp.arange(length)[None, :]
    mixing = jnp.exp(jnp.where(causal[:, :, None], spread, -jnp.inf))
    intersection = jnp.dot(outputs_f, inputs_f.T, precision=precise)
    return (cumul, ending, mixing * intersection[:, :, None])


def forward_step(carried, pieces):
    values, cumul, ending, weights, inputs_f, outputs_f = pieces
    inner = jnp.einsum("sth,thp->shp", weights, values, precision=precise)
    outer = jnp.exp(cumul)[:, :, None] * jnp.einsum(
        "sn,hnp->shp", outputs_f, carried, precision=precise
    )
    fresh = jnp.einsum(
        "th,tn,thp->hnp", jnp.exp(ending[None, :] - cumul), inputs_f, values, precision=precise
    )
    return (jnp.exp(ending)[:, None, None] * carried + fresh, inner + outer)


def backward_step(carried, pieces):
    grads, cumul, ending, weights, inputs_f, outputs_f = pieces
    inner = jnp.einsum("sth,shp->thp", weights, grads, precision=precise)
    outer = jnp.exp(ending[None, :] - cumul)[:, :, None] * jnp.einsum(
        "tn,hnp->thp", inputs_f, carried, precision=precise
    )
    fresh = jnp.einsum("sh,sn,shp->hnp", jnp.exp(cumul), outputs_f, grads, precision=precise)
    return (jnp.exp(ending)[:, None, None] * carried + fresh, inner + outer)


def join_forward(earlier, later):
    return (earlier[0] * later[0], later[0][:, None, None] * earlier[1] + later[1])


def join_backward(earlier, later):
    return (earlier[0] * later[0], later[1] + later[0][:, None, None] * earlier[1])


def per_device(
    tokens, grad_out, in_weight, in_scale, out_weight, out_scale, state_in, state_out, log_decay
):
    local_rows = tokens.shape[0]
    heads_here = log_decay.shape[1]
    width_here = in_scale.shape[0]
    head_size = width_here // heads_here
    state_size = state_in.shape[1]
    weight_rows = in_weight.shape[0]
    blocks = local_rows // STRETCH
    row_start = lax.axis_index("seq") * weight_rows
    out_scale_rows = lax.dynamic_slice_in_dim(out_scale, row_start, weight_rows)
    in_levels, in_slopes, in_inside = quantize(in_weight, in_scale[None, :])
    out_levels, out_slopes, out_inside = quantize(out_weight, out_scale_rows[:, None])
    in_codes = lax.all_gather(in_levels.astype(jnp.bfloat16), "seq", axis=0, tiled=True)
    out_codes = lax.all_gather(out_levels.astype(jnp.bfloat16), "seq", axis=0, tiled=True)
    features = lax.all_gather(tokens, "tp", axis=1, tiled=True)
    cotangent = lax.all_gather(grad_out, "tp", axis=1, tiled=True)
    projected = jnp.dot(features, in_codes, preferred_element_type=jnp.float32) * in_scale[None, :]
    scaled_grad = (cotangent.astype(jnp.float32) * out_scale[None, :]).astype(jnp.bfloat16)
    grad_mixed = jnp.dot(scaled_grad, out_codes, preferred_element_type=jnp.float32)
    inputs_full = state_in.astype(jnp.float32)
    outputs_full = state_out.astype(jnp.float32)
    decay_blocks = log_decay.reshape(blocks, STRETCH, heads_here)
    input_blocks = inputs_full.reshape(blocks, STRETCH, state_size)
    output_blocks = outputs_full.reshape(blocks, STRETCH, state_size)
    cumul, ending, weights = jax.vmap(stretch_terms)(decay_blocks, input_blocks, output_blocks)
    value_blocks = projected.reshape(blocks, STRETCH, heads_here, head_size)
    grad_blocks = grad_mixed.reshape(blocks, STRETCH, heads_here, head_size)
    empty = jnp.zeros((heads_here, state_size, head_size), jnp.float32)
    local_state, mixed_local = lax.scan(
        forward_step, empty, (value_blocks, cumul, ending, weights, input_blocks, output_blocks)
    )
    local_grad_state, grad_local = lax.scan(
        backward_step,
        empty,
        (grad_blocks, cumul, ending, weights, input_blocks, output_blocks),
        reverse=True,
    )
    running = jnp.cumsum(log_decay, axis=0)
    device_total = running[-1]
    device_decay = jnp.exp(device_total)
    identity = (jnp.ones_like(device_decay), empty)
    entering = prefix((device_decay, local_state), "seq", join_forward, identity, False)[1]
    leaving = prefix((device_decay, local_grad_state), "seq", join_backward, identity, True)[1]
    mixed = mixed_local.reshape(local_rows, heads_here, head_size) + jnp.exp(running)[
        :, :, None
    ] * jnp.einsum("tn,hnp->thp", outputs_full, entering, precision=precise)
    grad_values = grad_local.reshape(local_rows, heads_here, head_size) + jnp.exp(
        device_total[None, :] - running
    )[:, :, None] * jnp.einsum("tn,hnp->thp", inputs_full, leaving, precision=precise)
    mixed = mixed.reshape(local_rows, width_here)
    grad_values = grad_values.reshape(local_rows, width_here)
    mixed_b = mixed.astype(jnp.bfloat16)
    grad_b = grad_values.astype(jnp.bfloat16)
    grad_scaled = (grad_values * in_scale[None, :]).astype(jnp.bfloat16)
    piece = features
    in_total = lax.psum_scatter(
        jnp.einsum("td,tc->dc", piece, grad_b, preferred_element_type=jnp.float32).astype(
            jnp.bfloat16
        ),
        "seq",
        scatter_dimension=0,
        tiled=True,
    ).astype(jnp.float32)
    piece = cotangent
    out_total = lax.psum_scatter(
        jnp.einsum("td,tc->dc", piece, mixed_b, preferred_element_type=jnp.float32).astype(
            jnp.bfloat16
        ),
        "seq",
        scatter_dimension=0,
        tiled=True,
    ).astype(jnp.float32)
    partial_tokens = jnp.einsum(
        "tc,dc->td", grad_scaled, in_codes, preferred_element_type=jnp.float32
    )
    grad_tokens = lax.psum_scatter(
        partial_tokens.astype(jnp.bfloat16), "tp", scatter_dimension=1, tiled=True
    )
    in_part = jnp.sum(in_total * in_slopes, axis=0)
    out_part = jnp.sum(out_total * out_slopes, axis=1)
    in_sum = lax.psum(in_part, "seq")
    out_sum = lax.psum(out_part, "tp")
    grad_in_scale = in_sum / jnp.sqrt(jnp.float32(D * QMAX))
    grad_out_scale = out_sum / jnp.sqrt(jnp.float32(HEADS * HEAD_DIM * QMAX))
    return (
        grad_tokens,
        in_total * in_inside,
        grad_in_scale,
        out_total * out_inside,
        grad_out_scale,
    )


def solution(mesh):
    placed = (
        P("seq", "tp"),
        P("seq", "tp"),
        P("seq", "tp"),
        P("tp"),
        P("seq", "tp"),
        P(),
        P("seq", None),
        P("seq", None),
        P("seq", "tp"),
    )
    return jax.shard_map(
        per_device,
        mesh=mesh,
        in_specs=placed,
        out_specs=(P("seq", "tp"), P("seq", "tp"), P("tp"), P("seq", "tp"), P("seq")),
        check_vma=False,
    )
```

profile of v0, /device:TPU:6, one launch (start us, length us, event | category | flops | bytes accessed | tf_op | source)
XLA Modules:
  0.0 612.6 jit_solution(15400213899961906926)
XLA Ops:
  8.0 1.0 copy.60
  10.5 1.3 reduce-window.14
  12.4 41.5 %all-gather.10.cloned.1.call-done = bf16[256,4096]{1,0:T(8,128)(2,1)} async-done(((bf16[256,512]{1,0:T(8,128)(2,1)}), bf16[256,4096]{1,0:T(8,128)(2,1)}) %all-gather.10.cloned.1.call-update) | async-done | bytes 2097168 | tf_op jit(solution)/shard_map/all_gather | solution.py:104
  53.9 55.4 %all-gather.12.cloned.1.call-done = bf16[4096,512]{0,1:T(8,128)(2,1)} async-done(((bf16[128,512]{0,1:T(8,128)(2,1)}), bf16[4096,512]{0,1:T(8,128)(2,1)}) %all-gather.12.cloned.1.call-update) | async-done | bytes 4194320 | tf_op jit(solution)/shard_map/all_gather | solution.py:102
  109.3 4.1 fusion.2
  113.4 1.0 fusion.20
  116.2 18.9 %all-gather.2 = bf16[32,1,8]{2,1,0:T(2,128)(2,1)S(1)} all-gather(bf16[1,1,8]{2,1,0:T(2,128)(2,1)S(1)} %bitcast.154), channel_id=1, replica_groups=mesh['seq'=32,'tp'=8] {'seq'}, dimensions={0}, use_global_device_ids=true | all-gather | bytes 528 | tf_op jit(solution)/shard_map/all_gather | solution.py:19
  135.6 1.8 fusion.6
  137.5 28.1 %all-gather.18.cloned.1.call-done = bf16[256,128,64]{1,2,0:T(8,128)(2,1)} async-done(((bf16[8,128,64]{1,2,0:T(8,128)(2,1)}), bf16[256,128,64]{1,2,0:T(8,128)(2,1)}) %all-gather.18.cloned.1.call-update) | async-done | bytes 4194320 | tf_op jit(solution)/shard_map/all_gather | solution.py:19
  165.6 32.6 %while.16 = (s32[]{:T(128)}, f32[8,128,64]{2,1,0:T(8,128)S(1)}, s32[]{:T(128)}, bf16[32,8,128,64]{2,3,1,0:T(8,128)(2,1)}, bf16[32,8]{1,0:T(8,128)(2,1)S(1)}, /*index=5*/s32[]{:T(128)}, s32[]{:T(128)}, s32[]{:T(128)}, s32[]{:T(128)}) while((s32[]{:T(128)}, f32[8,128,64]{2,1,0:T(8,128)S(1)}, s32[]{:T(128)}, bf16[32,8,128,64]{2,3,1,0:T(8,128)(2,1)}, ...), condition=%wide.region_5.6_spmd, body=%wide.region_4.5_spmd.sunk | while | flops 196622 | bytes 1179883 | solution.py:34
  165.6 0.9 constant_dynamic-slice_fusion.4
  166.9 0.9 constant_dynamic-slice_fusion.4
  168.2 0.9 constant_dynamic-slice_fusion.4
  170.8 0.9 constant_dynamic-slice_fusion.4
  172.1 0.9 constant_dynamic-slice_fusion.4
  173.4 0.9 constant_dynamic-slice_fusion.4
  174.7 0.9 constant_dynamic-slice_fusion.4
  177.3 0.9 constant_dynamic-slice_fusion.4
  179.9 0.9 constant_dynamic-slice_fusion.4
  181.3 0.9 constant_dynamic-slice_fusion.4
  182.6 0.9 constant_dynamic-slice_fusion.4
  183.9 0.9 constant_dynamic-slice_fusion.4
  185.2 0.9 constant_dynamic-slice_fusion.4
  187.8 0.9 constant_dynamic-slice_fusion.4
  189.1 0.9 constant_dynamic-slice_fusion.4
  191.7 0.9 constant_dynamic-slice_fusion.4
  193.0 0.9 constant_dynamic-slice_fusion.4
  195.6 0.9 constant_dynamic-slice_fusion.4
  196.9 0.9 constant_dynamic-slice_fusion.4
  199.3 8.6 %all-gather.16.cloned.1.call-done = bf16[256,4096]{1,0:T(8,128)(2,1)} async-done(((bf16[256,512]{1,0:T(8,128)(2,1)}), bf16[256,4096]{1,0:T(8,128)(2,1)}) %all-gather.16.cloned.1.call-update) | async-done | bytes 2097168 | tf_op jit(solution)/shard_map/all_gather | solution.py:103
  207.9 4.8 fusion
  212.7 6.5 %copy.81 = bf16[4096,512]{1,0:T(8,128)(2,1)} copy(bf16[4096,512]{0,1:T(8,128)(2,1)} %fusion) | data formatting | bytes 8388608
  220.2 87.2 %reduce-scatter.10.cloned.1.call-done = bf16[128,512]{1,0:T(8,128)(2,1)} async-done(((bf16[4096,512]{1,0:T(8,128)(2,1)}), bf16[128,512]{1,0:T(8,128)(2,1)}) %reduce-scatter.10.cloned.1.call-update) | async-done | bytes 131088
  307.4 1.0 copy.82
  309.3 54.8 %all-gather.14.cloned.1.call-done = bf16[4096,512]{0,1:T(8,128)(2,1)} async-done(((bf16[128,512]{0,1:T(8,128)(2,1)}), bf16[4096,512]{0,1:T(8,128)(2,1)}) %all-gather.14.cloned.1.call-update) | async-done | bytes 4194320 | tf_op jit(solution)/shard_map/all_gather | solution.py:101
  364.1 3.5 convolution_multiply_fusion
  368.4 1.0 fusion.19
  369.6 3.5 fusion.7
  373.0 47.4 %all-gather.20.cloned.1.call-done = bf16[256,128,64]{1,2,0:T(8,128)(2,1)} async-done(((bf16[8,128,64]{1,2,0:T(8,128)(2,1)}), bf16[256,128,64]{1,2,0:T(8,128)(2,1)}) %all-gather.20.cloned.1.call-update) | async-done | bytes 4194320 | tf_op jit(solution)/shard_map/all_gather | solution.py:19
  420.5 8.0 %while.17 = (s32[]{:T(128)}, f32[8,128,64]{2,1,0:T(8,128)S(1)}, s32[]{:T(128)}, bf16[32,8]{1,0:T(8,128)(2,1)S(1)}, bf16[32,8,128,64]{2,3,1,0:T(8,128)(2,1)}, /*index=5*/s32[]{:T(128)}, s32[]{:T(128)}, s32[]{:T(128)}) while((s32[]{:T(128)}, f32[8,128,64]{2,1,0:T(8,128)S(1)}, s32[]{:T(128)}, bf16[32,8]{1,0:T(8,128)(2,1)S(1)}, ...), condition=%wide.region_11.12_spmd, body=%wide.region_10.11_spmd.sunk | while | flops 196621 | bytes 1179863 | solution.py:34
  430.1 3.2 fusion.1
  433.4 6.5 %copy.83 = bf16[4096,512]{1,0:T(8,128)(2,1)} copy(bf16[4096,512]{0,1:T(8,128)(2,1)} %fusion.1) | data formatting | bytes 8388608
  440.1 4.9 convolution_convert_fusion.2
  445.8 83.4 %psum.14 = f32[512]{0:T(512)S(1)} all-reduce(f32[512]{0:T(512)S(1)} %get-tuple-element.273), channel_id=1, replica_groups=mesh['seq'=32,'tp'=8] {'seq'}, use_global_device_ids=true, to_apply=%region_9.10 | all-reduce | flops 512 | bytes 4096 | tf_op jit(solution)/shard_map/psum | solution.py:169
  529.8 31.0 %reduce-scatter.12.cloned.1.call-done = bf16[128,512]{1,0:T(8,128)(2,1)} async-done(((bf16[4096,512]{1,0:T(8,128)(2,1)}), bf16[128,512]{1,0:T(8,128)(2,1)}) %reduce-scatter.12.cloned.1.call-update) | async-done | bytes 131088
  560.8 1.0 copy.84
  562.8 17.4 %psum.15 = f32[128]{0:T(128)S(1)} all-reduce(f32[128]{0:T(128)S(1)} %get-tuple-element.275), channel_id=1, replica_groups=mesh['seq'=32,'tp'=8] {'tp'}, use_global_device_ids=true, to_apply=%region_14.15 | all-reduce | flops 128 | bytes 1024 | tf_op jit(solution)/shard_map/psum | solution.py:170
  580.7 25.3 %reduce-scatter.8.cloned.1.call-done = bf16[256,512]{1,0:T(8,128)(2,1)} async-done(((bf16[256,4096]{1,0:T(8,128)(2,1)}), bf16[256,512]{1,0:T(8,128)(2,1)}) %reduce-scatter.8.cloned.1.call-update) | async-done | bytes 262160 | tf_op jit(solution)/shard_map/reduce_scatter | solution.py:164
  (179 shorter events, 35.4 us)
Async XLA Ops:
  7.2 128.3 %copy-start = (bf16[256,128]{1,0:T(8,128)(2,1)S(1)}, bf16[256,128]{1,0:T(8,128)(2,1)}, u32[]{:S(2)}) copy-start(bf16[256,128]{1,0:T(8,128)(2,1)} %param.19) | copy-start | bytes 196612
  7.2 46.7 %all-gather.10.cloned.1.call-start = ((), (), s32[]{:S(2)}) async-start(), calls=%async_computation.3 | async-start | bytes 2359296 | tf_op jit(solution)/shard_map/all_gather | solution.py:104
  7.9 101.4 %all-gather.12.cloned.1.call-start = ((), (), s32[]{:S(2)}) async-start(), calls=%async_computation.4 | async-start | bytes 4325376 | tf_op jit(solution)/shard_map/all_gather | solution.py:102
  10.5 155.0 %all-gather.18.cloned.1.call-start = ((), (), s32[]{:S(2)}) async-start(), calls=%async_computation.8 | async-start | bytes 4325376 | tf_op jit(solution)/shard_map/all_gather | solution.py:19
  12.4 101.1 %copy-start.3 = (bf16[256,128]{1,0:T(8,128)(2,1)S(1)}, bf16[256,128]{1,0:T(8,128)(2,1)}, u32[]{:S(2)}) copy-start(bf16[256,128]{1,0:T(8,128)(2,1)} %param.20) | copy-start | bytes 196612
  12.4 102.8 %copy-start.8 = (f32[256,8]{0,1:T(8,128)S(1)}, f32[256,8]{0,1:T(8,128)}, u32[]{:S(2)}) copy-start(f32[256,8]{0,1:T(8,128)} %param.21) | copy-start | bytes 24580
  114.5 93.4 %all-gather.16.cloned.1.call-start = ((), (), s32[]{:S(2)}) async-start(), calls=%async_computation.7 | async-start | bytes 2359296 | tf_op jit(solution)/shard_map/all_gather | solution.py:103
  115.1 192.3 %reduce-scatter.10.cloned.1.call-start = ((), (), s32[]{:S(2)}) async-start(), calls=%async_computation.10 | async-start | bytes 4325376
  135.6 30.0 %copy-start.5 = (f32[256,256]{1,0:T(8,128)}, f32[256,256]{1,0:T(8,128)S(1)}, u32[]{:S(2)}) copy-start(f32[256,256]{1,0:T(8,128)S(1)} %fusion.57) | copy-start | bytes 786436
  219.2 0.9 copy-start.7
  219.2 89.2 %copy-start.9 = (f32[512]{0:T(512)S(1)}, f32[512]{0:T(512)}, u32[]{:S(2)}) copy-start(f32[512]{0:T(512)} %param.16) | copy-start | bytes 6148
  219.2 145.0 %copy-start.2 = (bf16[256,4096]{1,0:T(8,128)(2,1)S(1)}, bf16[256,4096]{1,0:T(8,128)(2,1)}, u32[]{:S(2)}) copy-start(bf16[256,4096]{1,0:T(8,128)(2,1)} %all-gather.16.cloned.1.call-done) | copy-start | bytes 6291460
  219.2 145.0 %all-gather.14.cloned.1.call-start = ((), (), s32[]{:S(2)}) async-start(), calls=%async_computation.5 | async-start | bytes 4325376 | tf_op jit(solution)/shard_map/all_gather | solution.py:101
  309.3 60.3 %copy-start.6 = (f32[256,256]{1,0:T(8,128)S(1)}, f32[256,256]{1,0:T(8,128)}, u32[]{:S(2)}) copy-start(f32[256,256]{1,0:T(8,128)} %copy-done.5) | copy-start | bytes 786436
  309.3 111.2 %all-gather.20.cloned.1.call-start = ((), (), s32[]{:S(2)}) async-start(), calls=%async_computation.9 | async-start | bytes 4325376 | tf_op jit(solution)/shard_map/all_gather | solution.py:19
  367.6 0.8 copy-start.4
  369.5 191.3 %reduce-scatter.12.cloned.1.call-start = ((), (), s32[]{:S(2)}) async-start(), calls=%async_computation.11 | async-start | bytes 4325376
  428.5 1.6 copy-start.1
  439.9 166.1 %reduce-scatter.8.cloned.1.call-start = ((), (), s32[]{:S(2)}) async-start(), calls=%async_computation.6 | async-start | bytes 2359296 | tf_op jit(solution)/shard_map/reduce_scatter | solution.py:164
Sparse Core Ops, SparseCore 0:
  9.8 44.0 all-gather.9
  56.9 52.3 all-gather.11
  114.6 50.8 all-gather.17
  167.2 40.6 all-gather.15
  219.3 88.0 reduce-scatter.9
  310.6 53.5 all-gather.13
  369.6 50.7 all-gather.19
  440.0 120.7 reduce-scatter.11
  563.9 42.0 reduce-scatter.7
where the time goes:
time: 614 us; the launch traced here: 613 us
  waiting for transfers between devices  381 us (62%)
  blocking collectives  120 us (20%)
  local copies, waits for them, and re-layouts  55.6 us (9%)
  matrix products  30.2 us (5%)
  between operations  14.1 us (2%)
  other arithmetic  10.6 us (2%)
    unnamed x11, waiting for transfers between devices  119 us
    psum x1, blocking collectives, per_device(): in_sum = lax.psum(in_part, 'seq')  83.4 us
    all_gather x2, waiting for transfers between devices, prefix(): lax.all_gather(a.astype(kind), axis)  75.5 us
    all_gather x1, waiting for transfers between devices, per_device(): lax.all_gather(out_levels.astype(jnp.bfloat16), 'seq', axis=0, tiled=True)  55.4 us
    all_gather x1, waiting for transfers between devices, per_device(): lax.all_gather(in_levels.astype(jnp.bfloat16), 'seq', axis=0, tiled=True)  54.8 us
    all_gather x1, waiting for transfers between devices, per_device(): cotangent = lax.all_gather(grad_out, 'tp', axis=1, tiled=True)  41.5 us
    dynamic_slice x62, local copies, waits for them, and re-layouts, one(): lax.dynamic_index_in_dim(a, source, 0, False).astype(own.dtype)  34 us
    reduce_scatter x1, waiting for transfers between devices, per_device(): lax.psum_scatter(partial_tokens.astype(jnp.bfloat16), 'tp', scatter_dimen...  25.3 us
  transfers between devices with their start and end apart: 9, of which 9 were waited for; matrix products, arithmetic and copies ran while one was open for 9% of the time, Pallas kernels for 0%

commit v1 on v0

--- a/solution.py
+++ b/solution.py
@@ -9,6 +9,19 @@
 STRETCH = 256
 QMAX = 7
 precise = lax.Precision.HIGHEST
+
+
+def ring_gather(x, axis, dim):
+    ways = lax.axis_size(axis)
+    up = [(d, (d + 1) % ways) for d in range(ways)]
+    down = [(d, (d - 1) % ways) for d in range(ways)]
+    earlier, later = ([x], [x])
+    for _ in range(ways // 2):
+        earlier.append(lax.ppermute(earlier[-1], axis, up))
+    for _ in range((ways - 1) // 2):
+        later.append(lax.ppermute(later[-1], axis, down))
+    line = jnp.concatenate([*earlier[::-1], *later[1:]], axis=dim)
+    return jnp.roll(line, (lax.axis_index(axis) - ways // 2) * x.shape[dim], axis=dim)
 
 
 def prefix(array, axis, join, neutral, backward):
@@ -101,7 +114,7 @@
     in_codes = lax.all_gather(in_levels.astype(jnp.bfloat16), "seq", axis=0, tiled=True)
     out_codes = lax.all_gather(out_levels.astype(jnp.bfloat16), "seq", axis=0, tiled=True)
     features = lax.all_gather(tokens, "tp", axis=1, tiled=True)
-    cotangent = lax.all_gather(grad_out, "tp", axis=1, tiled=True)
+    cotangent = ring_gather(grad_out, "tp", 1)
     projected = jnp.dot(features, in_codes, preferred_element_type=jnp.float32) * in_scale[None, :]
     scaled_grad = (cotangent.astype(jnp.float32) * out_scale[None, :]).astype(jnp.bfloat16)
     grad_mixed = jnp.dot(scaled_grad, out_codes, preferred_element_type=jnp.float32)

time: 614 us -> 567 us (0.923)
  waiting for transfers between devices: 381 us -> 313 us
  starting transfers between devices: 0.37 us -> 13 us
  local copies, waits for them, and re-layouts: 55.6 us -> 62.3 us
    all_gather x1, waiting for transfers between devices: 55.4 us -> 8.25 us  [per_device(): lax.all_gather(out_levels.astype(jnp.bfloat16), 'seq', axis=0, tiled=True)]
    all_gather x1 -> x0, waiting for transfers between devices: 41.5 us -> none  [per_device(): cotangent = lax.all_gather(grad_out, 'tp', axis=1, tiled=True)]
    ppermute x0 -> x7, waiting for transfers between devices: none -> 22.1 us  [the longest x4 22.1 us: ring_gather(): earlier.append(lax.ppermute(earlier[-1], axis, up))]
    ppermute x0 -> x7, starting transfers between devices: none -> 12.7 us  [the longest x3 10.6 us: ring_gather(): later.append(lax.ppermute(later[-1], axis, down))]
    unnamed x28 -> x44, local copies, waits for them, and re-layouts: 20.1 us -> 26 us
    unnamed x11 -> x10, waiting for transfers between devices: 119 us -> 119 us
  transfers between devices with their start and end apart: 9 -> 15, of which waited for: 9 -> 12; matrix products, arithmetic and copies ran while one was open for 9% -> 11% of each run, Pallas kernels for 0% -> 0%
where the time goes in v1:
time: 567 us; the launch traced here: 566 us
  waiting for transfers between devices  313 us (55%)
  blocking collectives  120 us (21%)
  local copies, waits for them, and re-layouts  62.3 us (11%)
  matrix products  31.8 us (6%)
  between operations  14.4 us (3%)
  starting transfers between devices  13 us (2%)
  other arithmetic  10.6 us (2%)
    unnamed x10, waiting for transfers between devices  119 us
    psum x1, blocking collectives, per_device(): in_sum = lax.psum(in_part, 'seq')  83.4 us
    all_gather x2, waiting for transfers between devices, prefix(): lax.all_gather(a.astype(kind), axis)  74.6 us
    all_gather x1, waiting for transfers between devices, per_device(): lax.all_gather(in_levels.astype(jnp.bfloat16), 'seq', axis=0, tiled=True)  54.8 us
    dynamic_slice x62, local copies, waits for them, and re-layouts, one(): lax.dynamic_index_in_dim(a, source, 0, False).astype(own.dtype)  34 us
    unnamed x44, local copies, waits for them, and re-layouts  26 us
    reduce_scatter x1, waiting for transfers between devices, per_device(): lax.psum_scatter(partial_tokens.astype(jnp.bfloat16), 'tp', scatter_dimen...  25 us
    ppermute x4, waiting for transfers between devices, ring_gather(): earlier.append(lax.ppermute(earlier[-1], axis, up))  22.1 us
  transfers between devices with their start and end apart: 15, of which 12 were waited for; matrix products, arithmetic and copies ran while one was open for 11% of the time, Pallas kernels for 0%

profile of v1, /device:TPU:6, one launch (start us, length us, event | category | flops | bytes accessed | tf_op | source)
XLA Modules:
  0.0 565.9 jit_solution(11866043661672841887)
XLA Ops:
  7.2 1.1 copy.63
  9.9 2.0 collective-permute-start
  11.9 4.0 collective-permute-start.4
  15.9 1.2 reduce-window.14
  17.1 5.2 collective-permute-done
  22.5 8.5 %collective-permute-done.1 = bf16[256,512]{1,0:T(8,128)(2,1)S(1)} collective-permute-done((bf16[256,512]{1,0:T(8,128)(2,1)S(1)}, bf16[256,512]{1,0:T(8,128)(2,1)S(1)}, u32[]{:S(2)}, u32[]{:S(2)}) %collective-permute-start.1) | collective-permute-done | bytes 262176 | tf_op jit(solution)/shard_map/ppermute | solution.py:20
  31.3 3.3 collective-permute-start.5
  34.6 4.3 collective-permute-done.2
  39.0 3.3 collective-permute-start.6
  42.4 4.1 collective-permute-done.3
  49.6 1.7 constant_dynamic-update-slice_fusion.11
  59.5 8.3 %all-gather.9.cloned.1.call-done = bf16[4096,512]{0,1:T(8,128)(2,1)} async-done(((bf16[128,512]{0,1:T(8,128)(2,1)}), bf16[4096,512]{0,1:T(8,128)(2,1)}) %all-gather.9.cloned.1.call-update) | async-done | bytes 4194320 | tf_op jit(solution)/shard_map/all_gather | solution.py:115
  67.8 4.1 fusion.1
  71.9 1.1 fusion.21
  74.9 18.9 %all-gather.2 = bf16[32,1,8]{2,1,0:T(2,128)(2,1)S(1)} all-gather(bf16[1,1,8]{2,1,0:T(2,128)(2,1)S(1)} %bitcast.151), channel_id=1, replica_groups=mesh['seq'=32,'tp'=8] {'seq'}, dimensions={0}, use_global_device_ids=true | all-gather | bytes 528 | tf_op jit(solution)/shard_map/all_gather | solution.py:32
  95.0 1.8 fusion.7
  96.8 27.2 %all-gather.15.cloned.1.call-done = bf16[256,128,64]{1,2,0:T(8,128)(2,1)} async-done(((bf16[8,128,64]{1,2,0:T(8,128)(2,1)}), bf16[256,128,64]{1,2,0:T(8,128)(2,1)}) %all-gather.15.cloned.1.call-update) | async-done | bytes 4194320 | tf_op jit(solution)/shard_map/all_gather | solution.py:32
  124.0 32.8 %while.16 = (s32[]{:T(128)}, f32[8,128,64]{2,1,0:T(8,128)S(1)}, s32[]{:T(128)}, bf16[32,8,128,64]{2,3,1,0:T(8,128)(2,1)}, bf16[32,8]{1,0:T(8,128)(2,1)S(1)}, /*index=5*/s32[]{:T(128)}, s32[]{:T(128)}, s32[]{:T(128)}, s32[]{:T(128)}) while((s32[]{:T(128)}, f32[8,128,64]{2,1,0:T(8,128)S(1)}, s32[]{:T(128)}, bf16[32,8,128,64]{2,3,1,0:T(8,128)(2,1)}, ...), condition=%wide.region_5.6_spmd, body=%wide.region_4.5_spmd.sunk | while | flops 196622 | bytes 1179883 | solution.py:47
  124.1 0.9 constant_dynamic-slice_fusion.4
  125.4 0.9 constant_dynamic-slice_fusion.4
  126.7 0.9 constant_dynamic-slice_fusion.4
  129.3 0.9 constant_dynamic-slice_fusion.4
  131.9 0.9 constant_dynamic-slice_fusion.4
  133.2 0.9 constant_dynamic-slice_fusion.4
  134.5 0.9 constant_dynamic-slice_fusion.4
  135.8 0.9 constant_dynamic-slice_fusion.4
  138.4 0.9 constant_dynamic-slice_fusion.4
  141.0 0.9 constant_dynamic-slice_fusion.4
  143.6 0.9 constant_dynamic-slice_fusion.4
  146.2 0.9 constant_dynamic-slice_fusion.4
  157.9 8.8 %all-gather.13.cloned.1.call-done = bf16[256,4096]{1,0:T(8,128)(2,1)} async-done(((bf16[256,512]{1,0:T(8,128)(2,1)}), bf16[256,4096]{1,0:T(8,128)(2,1)}) %all-gather.13.cloned.1.call-update) | async-done | bytes 2097168 | tf_op jit(solution)/shard_map/all_gather | solution.py:116
  166.8 4.8 fusion
  171.6 6.5 %copy.85 = bf16[4096,512]{1,0:T(8,128)(2,1)} copy(bf16[4096,512]{0,1:T(8,128)(2,1)} %fusion) | data formatting | bytes 8388608
  179.1 87.2 %reduce-scatter.10.cloned.1.call-done = bf16[128,512]{1,0:T(8,128)(2,1)} async-done(((bf16[4096,512]{1,0:T(8,128)(2,1)}), bf16[128,512]{1,0:T(8,128)(2,1)}) %reduce-scatter.10.cloned.1.call-update) | async-done | bytes 131088
  266.3 1.0 copy.86
  268.3 54.8 %all-gather.11.cloned.1.call-done = bf16[4096,512]{0,1:T(8,128)(2,1)} async-done(((bf16[128,512]{0,1:T(8,128)(2,1)}), bf16[4096,512]{0,1:T(8,128)(2,1)}) %all-gather.11.cloned.1.call-update) | async-done | bytes 4194320 | tf_op jit(solution)/shard_map/all_gather | solution.py:114
  323.1 3.5 convolution_multiply_fusion
  327.4 1.1 fusion.20
  328.5 3.5 fusion.8
  332.0 47.4 %all-gather.17.cloned.1.call-done = bf16[256,128,64]{1,2,0:T(8,128)(2,1)} async-done(((bf16[8,128,64]{1,2,0:T(8,128)(2,1)}), bf16[256,128,64]{1,2,0:T(8,128)(2,1)}) %all-gather.17.cloned.1.call-update) | async-done | bytes 4194320 | tf_op jit(solution)/shard_map/all_gather | solution.py:32
  379.4 7.8 %while.17 = (s32[]{:T(128)}, f32[8,128,64]{2,1,0:T(8,128)S(1)}, s32[]{:T(128)}, bf16[32,8]{1,0:T(8,128)(2,1)S(1)}, bf16[32,8,128,64]{2,3,1,0:T(8,128)(2,1)}, /*index=5*/s32[]{:T(128)}, s32[]{:T(128)}, s32[]{:T(128)}) while((s32[]{:T(128)}, f32[8,128,64]{2,1,0:T(8,128)S(1)}, s32[]{:T(128)}, bf16[32,8]{1,0:T(8,128)(2,1)S(1)}, ...), condition=%wide.region_11.12_spmd, body=%wide.region_10.11_spmd.sunk | while | flops 196621 | bytes 1179863 | solution.py:47
  388.3 4.9 convolution_convert_fusion
  393.4 4.9 convolution_convert_fusion.2
  399.1 83.4 %psum.14 = f32[512]{0:T(512)S(1)} all-reduce(f32[512]{0:T(512)S(1)} %get-tuple-element.273), channel_id=1, replica_groups=mesh['seq'=32,'tp'=8] {'seq'}, use_global_device_ids=true, to_apply=%region_9.10 | all-reduce | flops 512 | bytes 4096 | tf_op jit(solution)/shard_map/psum | solution.py:182
  483.1 31.0 %reduce-scatter.12.cloned.1.call-done = bf16[128,512]{1,0:T(8,128)(2,1)} async-done(((bf16[4096,512]{1,0:T(8,128)(2,1)}), bf16[128,512]{1,0:T(8,128)(2,1)}) %reduce-scatter.12.cloned.1.call-update) | async-done | bytes 131088
  514.1 1.0 copy.88
  516.1 17.4 %psum.15 = f32[128]{0:T(128)S(1)} all-reduce(f32[128]{0:T(128)S(1)} %get-tuple-element.275), channel_id=1, replica_groups=mesh['seq'=32,'tp'=8] {'tp'}, use_global_device_ids=true, to_apply=%region_14.15 | all-reduce | flops 128 | bytes 1024 | tf_op jit(solution)/shard_map/psum | solution.py:183
  534.0 25.0 %reduce-scatter.8.cloned.1.call-done = bf16[256,512]{1,0:T(8,128)(2,1)} async-done(((bf16[256,4096]{1,0:T(8,128)(2,1)}), bf16[256,512]{1,0:T(8,128)(2,1)}) %reduce-scatter.8.cloned.1.call-update) | async-done | bytes 262160 | tf_op jit(solution)/shard_map/reduce_scatter | solution.py:177
  (207 shorter events, 52.7 us)
Async XLA Ops:
  7.2 86.9 %copy-start = (bf16[256,128]{1,0:T(8,128)(2,1)S(1)}, bf16[256,128]{1,0:T(8,128)(2,1)}, u32[]{:S(2)}) copy-start(bf16[256,128]{1,0:T(8,128)(2,1)} %param.19) | copy-start | bytes 196612
  7.2 49.3 %copy-start.2 = (bf16[256,512]{1,0:T(8,128)(2,1)S(1)}, bf16[256,512]{1,0:T(8,128)(2,1)}, u32[]{:S(2)}) copy-start(bf16[256,512]{1,0:T(8,128)(2,1)} %param.14) | copy-start | bytes 786436
  7.2 60.6 %all-gather.9.cloned.1.call-start = ((), (), s32[]{:S(2)}) async-start(), calls=%async_computation.3 | async-start | bytes 4325376 | tf_op jit(solution)/shard_map/all_gather | solution.py:115
  9.8 114.2 %all-gather.15.cloned.1.call-start = ((), (), s32[]{:S(2)}) async-start(), calls=%async_computation.7 | async-start | bytes 4325376 | tf_op jit(solution)/shard_map/all_gather | solution.py:32
  9.9 12.5 %collective-permute-start = (bf16[256,512]{1,0:T(8,128)(2,1)}, bf16[256,512]{1,0:T(8,128)(2,1)S(1)}, u32[]{:S(2)}, u32[]{:S(2)}) collective-permute-start(bf16[256,512]{1,0:T(8,128)(2,1)} %param.14), channel_id=1, source_target_pairs={{0,1},{1,2},{2,3},{3,4},{4,5},{5,6},{6,7},{7,0},{8,9},{9,10},{10,1... | collective-permute-start | bytes 786440 | tf_op jit(solution)/shard_map/ppermute | solution.py:20
  11.9 19.4 %collective-permute-start.4 = (bf16[256,512]{1,0:T(8,128)(2,1)}, bf16[256,512]{1,0:T(8,128)(2,1)S(1)}, u32[]{:S(2)}, u32[]{:S(2)}) collective-permute-start(bf16[256,512]{1,0:T(8,128)(2,1)} %param.14), channel_id=1, source_target_pairs={{0,7},{1,0},{2,1},{3,2},{4,3},{5,4},{6,5},{7,6},{8,15},{9,8},{10,9... | collective-permute-start | bytes 786440 | tf_op jit(solution)/shard_map/ppermute | solution.py:22
  22.3 8.7 %collective-permute-start.1 = (bf16[256,512]{1,0:T(8,128)(2,1)S(1)}, bf16[256,512]{1,0:T(8,128)(2,1)S(1)}, u32[]{:S(2)}, u32[]{:S(2)}) collective-permute-start(bf16[256,512]{1,0:T(8,128)(2,1)S(1)} %collective-permute-done), channel_id=1, source_target_pairs={{0,1},{1,2},{2,3},{3,4},{4,5},{5,6},{6,7},{7,0},{8,9},{9,10},{10,1... | collective-permute-start | bytes 786440 | tf_op jit(solution)/shard_map/ppermute | solution.py:20
  31.0 7.9 %collective-permute-start.2 = (bf16[256,512]{1,0:T(8,128)(2,1)S(1)}, bf16[256,512]{1,0:T(8,128)(2,1)S(1)}, u32[]{:S(2)}, u32[]{:S(2)}) collective-permute-start(bf16[256,512]{1,0:T(8,128)(2,1)S(1)} %collective-permute-done.1), channel_id=1, source_target_pairs={{0,1},{1,2},{2,3},{3,4},{4,5},{5,6},{6,7},{7,0},{8,9},{9,10},{10,1... | collective-permute-start | bytes 786440 | tf_op jit(solution)/shard_map/ppermute | solution.py:20
  31.3 7.7 %collective-permute-start.5 = (bf16[256,512]{1,0:T(8,128)(2,1)S(1)}, bf16[256,512]{1,0:T(8,128)(2,1)S(1)}, u32[]{:S(2)}, u32[]{:S(2)}) collective-permute-start(bf16[256,512]{1,0:T(8,128)(2,1)S(1)} %collective-permute-done.4), channel_id=1, source_target_pairs={{0,7},{1,0},{2,1},{3,2},{4,3},{5,4},{6,5},{7,6},{8,15},{9,8},{10,9... | collective-permute-start | bytes 786440 | tf_op jit(solution)/shard_map/ppermute | solution.py:22
  38.9 7.6 %collective-permute-start.3 = (bf16[256,512]{1,0:T(8,128)(2,1)S(1)}, bf16[256,512]{1,0:T(8,128)(2,1)S(1)}, u32[]{:S(2)}, u32[]{:S(2)}) collective-permute-start(bf16[256,512]{1,0:T(8,128)(2,1)S(1)} %collective-permute-done.2), channel_id=1, source_target_pairs={{0,1},{1,2},{2,3},{3,4},{4,5},{5,6},{6,7},{7,0},{8,9},{9,10},{10,1... | collective-permute-start | bytes 786440 | tf_op jit(solution)/shard_map/ppermute | solution.py:20
  39.0 28.8 %copy-start.10 = (f32[4096]{0:T(1024)S(1)}, f32[4096]{0:T(1024)}, u32[]{:S(2)}) copy-start(f32[4096]{0:T(1024)} %param.18) | copy-start | bytes 49156
  39.0 13.7 %collective-permute-start.6 = (bf16[256,512]{1,0:T(8,128)(2,1)S(1)}, bf16[256,512]{1,0:T(8,128)(2,1)S(1)}, u32[]{:S(2)}, u32[]{:S(2)}) collective-permute-start(bf16[256,512]{1,0:T(8,128)(2,1)S(1)} %collective-permute-done.5), channel_id=1, source_target_pairs={{0,7},{1,0},{2,1},{3,2},{4,3},{5,4},{6,5},{7,6},{8,15},{9,8},{10,9... | collective-permute-start | bytes 786440 | tf_op jit(solution)/shard_map/ppermute | solution.py:22
  59.5 12.4 %copy-start.3 = (bf16[256,128]{1,0:T(8,128)(2,1)S(1)}, bf16[256,128]{1,0:T(8,128)(2,1)}, u32[]{:S(2)}) copy-start(bf16[256,128]{1,0:T(8,128)(2,1)} %param.20) | copy-start | bytes 196612
  59.5 14.2 %copy-start.8 = (f32[256,8]{0,1:T(8,128)S(1)}, f32[256,8]{0,1:T(8,128)}, u32[]{:S(2)}) copy-start(f32[256,8]{0,1:T(8,128)} %param.21) | copy-start | bytes 24580
  73.0 93.7 %all-gather.13.cloned.1.call-start = ((), (), s32[]{:S(2)}) async-start(), calls=%async_computation.6 | async-start | bytes 2359296 | tf_op jit(solution)/shard_map/all_gather | solution.py:116
  73.7 192.5 %reduce-scatter.10.cloned.1.call-start = ((), (), s32[]{:S(2)}) async-start(), calls=%async_computation.9 | async-start | bytes 4325376
  94.3 0.7 copy-start.5
  178.0 0.9 copy-start.7
  178.0 89.3 %copy-start.9 = (f32[512]{0:T(512)S(1)}, f32[512]{0:T(512)}, u32[]{:S(2)}) copy-start(f32[512]{0:T(512)} %param.16) | copy-start | bytes 6148
  178.0 145.0 %copy-start.1 = (bf16[256,4096]{1,0:T(8,128)(2,1)S(1)}, bf16[256,4096]{1,0:T(8,128)(2,1)}, u32[]{:S(2)}) copy-start(bf16[256,4096]{1,0:T(8,128)(2,1)} %all-gather.13.cloned.1.call-done) | copy-start | bytes 6291460
  178.1 145.0 %all-gather.11.cloned.1.call-start = ((), (), s32[]{:S(2)}) async-start(), calls=%async_computation.4 | async-start | bytes 4325376 | tf_op jit(solution)/shard_map/all_gather | solution.py:114
  268.2 60.3 %copy-start.6 = (f32[256,256]{1,0:T(8,128)S(1)}, f32[256,256]{1,0:T(8,128)}, u32[]{:S(2)}) copy-start(f32[256,256]{1,0:T(8,128)} %copy-done.5) | copy-start | bytes 786436
  268.2 111.2 %all-gather.17.cloned.1.call-start = ((), (), s32[]{:S(2)}) async-start(), calls=%async_computation.8 | async-start | bytes 4325376 | tf_op jit(solution)/shard_map/all_gather | solution.py:32
  326.5 0.8 copy-start.4
  328.4 185.6 %reduce-scatter.12.cloned.1.call-start = ((), (), s32[]{:S(2)}) async-start(), calls=%async_computation.10 | async-start | bytes 4325376
  393.2 165.9 %reduce-scatter.8.cloned.1.call-start = ((), (), s32[]{:S(2)}) async-start(), calls=%async_computation.5 | async-start | bytes 2359296 | tf_op jit(solution)/shard_map/reduce_scatter | solution.py:177
Sparse Core Ops, SparseCore 0:
  11.1 56.6 all-gather.8
  73.1 50.8 all-gather.14
  125.8 40.8 all-gather.12
  178.2 88.0 reduce-scatter.9
  269.5 53.5 all-gather.10
  328.6 50.7 all-gather.16
  393.3 120.6 reduce-scatter.11
  517.2 41.8 reduce-scatter.7
